TPU v7x, 32 devices: a whole 2x2x4 slice. The times are simulated.
32 devices in a mesh: rep: 16 (over z, x, core), fsdp: 2 (over y).
Axes of the slice: x: 2, y: 2, z: 4, core: 2. Of those that a mesh axis runs over, the one named last changes fastest.
Arguments:
- tokens: bfloat16 [31520, 512], P(('rep', 'fsdp')), may hold values from -6 to 6
- cotangent: bfloat16 [31520, 512], P(('rep', 'fsdp')), may hold values from -6 to 6
- routes: int32 [31520, 2], P(('rep', 'fsdp')), may hold values from 0 to 31, all different within a row
- image_count: int32 [32], P(('rep', 'fsdp')), may hold values from 2 to 5, as said below
- capacity: int32 [32], P(('rep', 'fsdp')), may hold values from 40 to 80, as said below
- norm1_gain: bfloat16 [512], P('fsdp'), may hold values from 0.5 to 1.5
- norm1_bias: bfloat16 [512], P('fsdp'), may hold values from -1.25 to 1.25
- w_qkv: bfloat16 [512, 1536], P('fsdp'), may hold values from -0.25 to 0.25
- bias_q: bfloat16 [512], P('fsdp'), may hold values from -1.25 to 1.25
- bias_v: bfloat16 [512], P('fsdp'), may hold values from -1.25 to 1.25
- w_out: bfloat16 [512, 512], P('fsdp'), may hold values from -0.75 to 0.75
- bias_out: bfloat16 [512], P('fsdp'), may hold values from -0.625 to 0.625
- norm2_gain: bfloat16 [512], P('fsdp'), may hold values from 0.5 to 1.5
- norm2_bias: bfloat16 [512], P('fsdp'), may hold values from -1.25 to 1.25
- w_router: bfloat16 [512, 32], P('fsdp'), may hold values from -0.1875 to 0.1875
- expert_in: bfloat16 [32, 512, 2048], P('fsdp'), may hold values from -0.25 to 0.25
- expert_in_bias: bfloat16 [32, 2048], P('fsdp'), may hold values from -1.25 to 1.25
- expert_out: bfloat16 [32, 2048, 512], P('fsdp'), may hold values from -0.1875 to 0.1875
- expert_out_bias: bfloat16 [32, 512], P('fsdp'), may hold values from -0.625 to 0.625
Outputs:
- outputs: bfloat16 [31520, 512], P(('rep', 'fsdp'))
- grad_tokens: float32 [31520, 512], P(('rep', 'fsdp'))
- balance_loss: float32 [], replicated
- grad_norm1_gain: float32 [512], P('fsdp')
- grad_norm1_bias: float32 [512], P('fsdp')
- grad_w_qkv: float32 [512, 1536], P('fsdp')
- grad_bias_q: float32 [512], P('fsdp')
- grad_bias_v: float32 [512], P('fsdp')
- grad_w_out: float32 [512, 512], P('fsdp')
- grad_bias_out: float32 [512], P('fsdp')
- grad_norm2_gain: float32 [512], P('fsdp')
- grad_norm2_bias: float32 [512], P('fsdp')
- grad_w_router: float32 [512, 32], P('fsdp')
- grad_expert_in: float32 [32, 512, 2048], P('fsdp', None, 'rep')
- grad_expert_in_bias: float32 [32, 2048], P('fsdp', 'rep')
- grad_expert_out: float32 [32, 2048, 512], P('fsdp', 'rep')
- grad_expert_out_bias: float32 [32, 512], P('fsdp', 'rep')
Inputs may be any that keep to these rules, and one draw needn't show every extreme that they name: `image_count`: every device holds at least one image; some device holds 5. `capacity`: some device may fill 80 slots of each expert.
All inputs are finite; a program needn't handle non-finite values.
Results may differ from a plain program's by a relative error of at most 0.015.
Values may be sent and summed in bfloat16 or wider, within the bound.
A program may use at most 384 MiB of HBM per device.

v0:
```python
import jax
import jax.numpy as jnp
from jax import lax
from jax.sharding import PartitionSpec as P

HEADS = 8
HEAD_DIM = 64
EXPERTS = 32
IMG_TOK = 197
CAP = 80


def norm_rows(values, norm_gain, offset):
    average = jnp.mean(values, axis=-1, keepdims=True)
    centred = values - average
    variance = jnp.mean(centred * centred, axis=-1, keepdims=True)
    return centred * lax.rsqrt(variance + 1e-06) * norm_gain + offset


def slot_table(choices, alive_mask, limit, row_total):
    pair_expert = jnp.concatenate([choices[:, 0], choices[:, 1]])
    live_pairs = jnp.concatenate([alive_mask, alive_mask])
    expert_ids = jnp.arange(EXPERTS, dtype=jnp.int32)
    onehot = ((pair_expert[:, None] == expert_ids[None, :]) & live_pairs[:, None]).astype(jnp.int32)
    before = jnp.cumsum(onehot, axis=0) - onehot
    position = jnp.sum(before * onehot, axis=1)
    kept_pairs = live_pairs & (position < limit)
    pair_slot = pair_expert * CAP + position
    pair_token = jnp.concatenate(
        [jnp.arange(row_total, dtype=jnp.int32), jnp.arange(row_total, dtype=jnp.int32)]
    )
    slot_owner = jnp.full((EXPERTS * CAP,), row_total, jnp.int32)
    target = jnp.where(kept_pairs, pair_slot, EXPERTS * CAP)
    slot_owner = slot_owner.at[target].set(pair_token, mode="drop")
    safe_slot = jnp.where(kept_pairs, pair_slot, 0)
    return (slot_owner, kept_pairs, safe_slot, target, onehot)


def shards(
    tokens,
    cotangent,
    routes,
    image_count,
    capacity,
    norm1_gain,
    norm1_bias,
    w_qkv,
    bias_q,
    bias_v,
    w_out,
    bias_out,
    norm2_gain,
    norm2_bias,
    w_router,
    expert_in,
    expert_in_bias,
    expert_out,
    expert_out_bias,
):
    rows_count = tokens.shape[0]
    model_width = tokens.shape[1]
    image_total = rows_count // IMG_TOK
    score_scale = HEAD_DIM ** (-0.5)
    image_rows = jnp.arange(rows_count, dtype=jnp.int32) // IMG_TOK
    alive_mask = image_rows < image_count[0]
    alive_float = alive_mask.astype(jnp.float32)[:, None]
    slot_owner, kept_pairs, safe_slot, target, onehot = slot_table(
        routes, alive_mask, capacity[0], rows_count
    )
    kept_float = kept_pairs.astype(jnp.float32)
    load_local = jnp.sum(onehot.astype(jnp.float32), axis=0)
    live_local = jnp.sum(alive_float)
    load_total, live_total = lax.psum((load_local, live_local), ("rep", "fsdp"))
    gathered = (
        lax.all_gather(norm1_gain, "fsdp", axis=0, tiled=True),
        lax.all_gather(norm1_bias, "fsdp", axis=0, tiled=True),
        lax.all_gather(w_qkv, "fsdp", axis=0, tiled=True),
        lax.all_gather(bias_q, "fsdp", axis=0, tiled=True),
        lax.all_gather(bias_v, "fsdp", axis=0, tiled=True),
        lax.all_gather(w_out, "fsdp", axis=0, tiled=True),
        lax.all_gather(bias_out, "fsdp", axis=0, tiled=True),
        lax.all_gather(norm2_gain, "fsdp", axis=0, tiled=True),
        lax.all_gather(norm2_bias, "fsdp", axis=0, tiled=True),
        lax.all_gather(w_router, "fsdp", axis=0, tiled=True),
    )
    (
        gain_one,
        shift_one,
        qkv_full,
        query_bias,
        value_bias,
        out_full,
        out_bias,
        gain_two,
        shift_two,
        router_full,
    ) = gathered
    gain_one = gain_one.astype(jnp.float32)
    shift_one = shift_one.astype(jnp.float32)
    gain_two = gain_two.astype(jnp.float32)
    shift_two = shift_two.astype(jnp.float32)
    inputs = tokens.astype(jnp.float32)
    normed = norm_rows(inputs, gain_one, shift_one)
    normed_low = normed.astype(jnp.bfloat16)
    bias_row = jnp.concatenate([query_bias, jnp.zeros_like(query_bias), value_bias]).astype(
        jnp.float32
    )
    packed_low = (
        jnp.dot(normed_low, qkv_full, preferred_element_type=jnp.float32) + bias_row
    ).astype(jnp.bfloat16)
    image_shape = (image_total, IMG_TOK, HEADS, HEAD_DIM)
    queries = packed_low[:, :model_width].reshape(image_shape)
    all_keys = packed_low[:, model_width : 2 * model_width].reshape(image_shape)
    valued = packed_low[:, 2 * model_width :].reshape(image_shape)

    def score_block():
        return (
            jnp.einsum("iqhd,ikhd->hiqk", queries, all_keys, preferred_element_type=jnp.float32)
            * score_scale
        )

    scores = score_block()
    row_peak = jnp.max(scores, axis=-1, keepdims=True)
    exp_scores = jnp.exp(scores - row_peak)
    totals = jnp.sum(exp_scores, axis=-1, keepdims=True)
    log_total = row_peak + jnp.log(totals)
    attn_low = (exp_scores / totals).astype(jnp.bfloat16)
    mixed_low = (
        jnp.einsum("hiqk,ikhd->iqhd", attn_low, valued, preferred_element_type=jnp.float32)
        .reshape(rows_count, model_width)
        .astype(jnp.bfloat16)
    )
    middle = (
        inputs
        + jnp.dot(mixed_low, out_full, preferred_element_type=jnp.float32)
        + out_bias.astype(jnp.float32)
    )
    second_low = norm_rows(middle, gain_two, shift_two).astype(jnp.bfloat16)
    logits = jnp.dot(second_low, router_full, preferred_element_type=jnp.float32)
    expert_ids = jnp.arange(EXPERTS, dtype=jnp.int32)
    first_hot = (routes[:, 0:1] == expert_ids[None, :]).astype(jnp.float32)
    second_hot = (routes[:, 1:2] == expert_ids[None, :]).astype(jnp.float32)

    def gate_terms(logit_rows):
        router_probs = jax.nn.softmax(logit_rows, axis=-1)
        pick_one = jnp.sum(router_probs * first_hot, axis=-1)
        pick_two = jnp.sum(router_probs * second_hot, axis=-1)
        pick_total = pick_one + pick_two
        return (pick_one / pick_total, pick_two / pick_total, router_probs)

    (gate_first, gate_second, router_probs), gate_back = jax.vjp(gate_terms, logits)
    padded_rows = jnp.concatenate([second_low, jnp.zeros((1, model_width), jnp.bfloat16)], axis=0)
    sent_rows = padded_rows[slot_owner].reshape(EXPERTS, CAP, model_width)
    received = lax.all_to_all(sent_rows, "fsdp", split_axis=0, concat_axis=1, tiled=True)
    raised = (
        jnp.einsum("esd,edf->esf", received, expert_in, preferred_element_type=jnp.float32)
        + expert_in_bias.astype(jnp.float32)[:, None, :]
    )
    active, gelu_back = jax.vjp(jax.nn.gelu, raised)
    active_low = active.astype(jnp.bfloat16)
    produced = (
        jnp.einsum("esf,efd->esd", active_low, expert_out, preferred_element_type=jnp.float32)
        + expert_out_bias.astype(jnp.float32)[:, None, :]
    ).astype(jnp.bfloat16)
    returned = lax.all_to_all(produced, "fsdp", split_axis=1, concat_axis=0, tiled=True).reshape(
        EXPERTS * CAP, model_width
    )
    pair_rows = returned[safe_slot].astype(jnp.float32)
    pair_weight = jnp.concatenate([gate_first, gate_second]) * kept_float
    expert_sum = jnp.sum(
        (pair_rows * pair_weight[:, None]).reshape(2, rows_count, model_width), axis=0
    )
    outputs = (alive_float * (middle + expert_sum)).astype(jnp.bfloat16)
    upstream = cotangent.astype(jnp.float32) * alive_float
    pair_grad = jnp.concatenate([upstream, upstream], axis=0)
    gate_grads = jnp.sum(pair_grad * pair_rows, axis=1) * kept_float
    slot_gate = jnp.zeros((EXPERTS * CAP,), jnp.float32).at[target].set(pair_weight, mode="drop")
    padded_grad = jnp.concatenate([upstream, jnp.zeros((1, model_width), jnp.float32)], axis=0)
    slot_grads = (
        (padded_grad[slot_owner] * slot_gate[:, None])
        .astype(jnp.bfloat16)
        .reshape(EXPERTS, CAP, model_width)
    )
    grad_received = lax.all_to_all(slot_grads, "fsdp", split_axis=0, concat_axis=1, tiled=True)
    grad_active = jnp.einsum(
        "esd,efd->esf", grad_received, expert_out, preferred_element_type=jnp.float32
    )
    (grad_raised,) = gelu_back(grad_active)
    grad_raised_low = grad_raised.astype(jnp.bfloat16)
    grad_rows = jnp.einsum(
        "esf,edf->esd", grad_raised_low, expert_in, preferred_element_type=jnp.float32
    ).astype(jnp.bfloat16)
    back_rows = lax.all_to_all(grad_rows, "fsdp", split_axis=1, concat_axis=0, tiled=True).reshape(
        EXPERTS * CAP, model_width
    )
    expert_part = jnp.sum(
        (back_rows[safe_slot].astype(jnp.float32) * kept_float[:, None]).reshape(
            2, rows_count, model_width
        ),
        axis=0,
    )
    local_in = jnp.einsum(
        "esd,esf->edf", received, grad_raised_low, preferred_element_type=jnp.float32
    )
    local_in_bias = jnp.sum(grad_raised_low.astype(jnp.float32), axis=1)
    local_out = jnp.einsum(
        "esf,esd->efd", active_low, grad_received, preferred_element_type=jnp.float32
    )
    local_out_bias = jnp.sum(grad_received.astype(jnp.float32), axis=1)
    grad_in_weight, grad_in_bias, grad_out_weight, grad_out_expert_bias = (
        lax.psum_scatter(local_in, "rep", scatter_dimension=2, tiled=True),
        lax.psum_scatter(local_in_bias, "rep", scatter_dimension=1, tiled=True),
        lax.psum_scatter(local_out, "rep", scatter_dimension=1, tiled=True),
        lax.psum_scatter(local_out_bias, "rep", scatter_dimension=1, tiled=True),
    )
    prob_local = jnp.sum(router_probs * alive_float, axis=0)
    prob_total = lax.psum(prob_local, ("rep", "fsdp"))
    share = load_total / (2.0 * live_total)
    balance_loss = EXPERTS * jnp.sum(share * prob_total / live_total)
    aux_grad = alive_float * (EXPERTS * share / live_total)[None, :]
    (grad_logits,) = gate_back((gate_grads[:rows_count], gate_grads[rows_count:], aux_grad))
    grad_logits_low = grad_logits.astype(jnp.bfloat16)
    grad_router = jnp.dot(second_low.T, grad_logits_low, preferred_element_type=jnp.float32)
    grad_second = (
        jnp.dot(grad_logits_low, router_full.T, preferred_element_type=jnp.float32) + expert_part
    )
    _, norm_two_back = jax.vjp(norm_rows, middle, gain_two, shift_two)
    grad_mid_norm, grad_gain_two, grad_shift_two = norm_two_back(grad_second)
    grad_middle = upstream + grad_mid_norm
    grad_att_low = grad_middle.astype(jnp.bfloat16)
    grad_out_proj = jnp.dot(mixed_low.T, grad_att_low, preferred_element_type=jnp.float32)
    grad_out_bias = jnp.sum(grad_att_low.astype(jnp.float32), axis=0)
    grad_mixed = (
        jnp.dot(grad_att_low, out_full.T, preferred_element_type=jnp.float32)
        .astype(jnp.bfloat16)
        .reshape(image_shape)
    )
    recomputed = jnp.exp(score_block() - log_total)
    grad_weights = jnp.einsum(
        "iqhd,ikhd->hiqk", grad_mixed, valued, preferred_element_type=jnp.float32
    )
    grad_values = jnp.einsum(
        "hiqk,iqhd->ikhd",
        recomputed.astype(jnp.bfloat16),
        grad_mixed,
        preferred_element_type=jnp.float32,
    )
    inner_sum = jnp.sum(grad_weights * recomputed, axis=-1, keepdims=True)
    grad_scores = (recomputed * (grad_weights - inner_sum)).astype(jnp.bfloat16)
    grad_queries = (
        jnp.einsum("hiqk,ikhd->iqhd", grad_scores, all_keys, preferred_element_type=jnp.float32)
        * score_scale
    )
    grad_keys = (
        jnp.einsum("hiqk,iqhd->ikhd", grad_scores, queries, preferred_element_type=jnp.float32)
        * score_scale
    )
    grad_packed_low = jnp.concatenate(
        [
            grad_queries.reshape(rows_count, model_width),
            grad_keys.reshape(rows_count, model_width),
            grad_values.reshape(rows_count, model_width),
        ],
        axis=1,
    ).astype(jnp.bfloat16)
    grad_qkv = jnp.dot(normed_low.T, grad_packed_low, preferred_element_type=jnp.float32)
    packed_sums = jnp.sum(grad_packed_low.astype(jnp.float32), axis=0)
    grad_query_bias = packed_sums[:model_width]
    grad_value_bias = packed_sums[2 * model_width :]
    grad_normed = jnp.dot(grad_packed_low, qkv_full.T, preferred_element_type=jnp.float32)
    _, norm_one_back = jax.vjp(norm_rows, inputs, gain_one, shift_one)
    grad_input_norm, grad_gain_one, grad_shift_one = norm_one_back(grad_normed)
    grad_tokens = grad_middle + grad_input_norm
    local_grads = (
        grad_gain_one,
        grad_shift_one,
        grad_qkv,
        grad_query_bias,
        grad_value_bias,
        grad_out_proj,
        grad_out_bias,
        grad_gain_two,
        grad_shift_two,
        grad_router,
    )
    shares = (
        lax.psum_scatter(local_grads[0], "fsdp", scatter_dimension=0, tiled=True),
        lax.psum_scatter(local_grads[1], "fsdp", scatter_dimension=0, tiled=True),
        lax.psum_scatter(local_grads[2], "fsdp", scatter_dimension=0, tiled=True),
        lax.psum_scatter(local_grads[3], "fsdp", scatter_dimension=0, tiled=True),
        lax.psum_scatter(local_grads[4], "fsdp", scatter_dimension=0, tiled=True),
        lax.psum_scatter(local_grads[5], "fsdp", scatter_dimension=0, tiled=True),
        lax.psum_scatter(local_grads[6], "fsdp", scatter_dimension=0, tiled=True),
        lax.psum_scatter(local_grads[7], "fsdp", scatter_dimension=0, tiled=True),
        lax.psum_scatter(local_grads[8], "fsdp", scatter_dimension=0, tiled=True),
        lax.psum_scatter(local_grads[9], "fsdp", scatter_dimension=0, tiled=True),
    )
    owned = lax.psum(
        (
            shares[0],
            shares[1],
            shares[2],
            shares[3],
            shares[4],
            shares[5],
            shares[6],
            shares[7],
            shares[8],
            shares[9],
        ),
        "rep",
    )
    return (
        (outputs, grad_tokens, balance_loss)
        + tuple(owned)
        + (grad_in_weight, grad_in_bias, grad_out_weight, grad_out_expert_bias)
    )


def solution(mesh):
    in_specs = (
        P(("rep", "fsdp"), None),
        P(("rep", "fsdp"), None),
        P(("rep", "fsdp"), None),
        P(("rep", "fsdp")),
        P(("rep", "fsdp")),
        P("fsdp"),
        P("fsdp"),
        P("fsdp", None),
        P("fsdp"),
        P("fsdp"),
        P("fsdp", None),
        P("fsdp"),
        P("fsdp"),
        P("fsdp"),
        P("fsdp", None),
        P("fsdp", None, None),
        P("fsdp", None),
        P("fsdp", None, None),
        P("fsdp", None),
    )
    out_specs = (
        P(("rep", "fsdp"), None),
        P(("rep", "fsdp"), None),
        P(),
        P("fsdp"),
        P("fsdp"),
        P("fsdp", None),
        P("fsdp"),
        P("fsdp"),
        P("fsdp", None),
        P("fsdp"),
        P("fsdp"),
        P("fsdp"),
        P("fsdp", None),
        P("fsdp", None, "rep"),
        P("fsdp", "rep"),
        P("fsdp", "rep", None),
        P("fsdp", "rep"),
    )
    return jax.shard_map(shards, mesh=mesh, in_specs=in_specs, out_specs=out_specs, check_vma=False)
```

profile of v0, /device:TPU:0, one launch (start us, length us, event | category | flops | bytes accessed | tf_op | source)
XLA Modules:
  0.0 2065.0 jit_solution(907946020569079509)
XLA Ops:
  10.4 9.1 reduce-window.6
  20.6 5.2 all-gather
  25.8 4.2 all-gather.1
  30.1 4.3 all-gather.2
  34.4 4.2 all-gather.3
  38.7 4.2 all-gather.4
  42.9 4.2 all-gather.5
  47.2 4.2 all-gather.6
  51.5 10.0 scatter_custom_fusion
  61.6 7.2 all_gather.35
  69.5 3.3 add_convert_fusion
  74.5 2.9 reshape.396
  77.5 4.1 reshape.398
  81.5 3.8 reshape.397
  85.3 3.8 multiply_reduce_fusion.1
  92.3 4.2 fusion.12
  98.4 3.2 copy.76
  108.9 8.2 gather_fusion
  117.1 4.2 all-to-all-start
  121.4 23.7 %all-to-all-done = bf16[32,80,512]{2,1,0:T(8,128)(2,1)S(1)} async-done(((bf16[32,80,512]{2,1,0:T(8,128)(2,1)}), bf16[32,80,512]{2,1,0:T(8,128)(2,1)S(1)}, u32[]{:S(2)}, u32[]{:S(2)}) %all-to-all-start) | async-done | bytes 2621472 | tf_op jit(solution)/shard_map/all_to_all | solution.py:154
  148.6 20.5 fusion.122
  169.0 25.9 %add_convert_fusion.1 = bf16[16,160,512]{2,1,0:T(8,128)(2,1)} fusion(f32[16,512]{1,0:T(8,128)S(1)} %convert_element_type.161, bf16[16,2048,512]{2,1,0:T(8,128)(2,1)} %param.36, f32[16,160,2048]{2,1,0:T(8,128)} %fusion.122, f32[16,2048]{1,0:T(8,128)S(1)} %convert_element_type.159), kind=kOutput, calls=%fused_computation.30 | convolution fusion | flops 5423759360 | bytes 57311232 | tf_op jit(solution)/shard_map/esf,efd->esd/dot_general | solution.py:162
  194.9 4.7 copy.80
  199.6 5.2 all-to-all-start.1
  206.6 7.5 gather_fusion.2
  214.1 13.9 all_gather.39
  228.7 3.2 copy.81
  231.9 9.1 gather_fusion.1
  241.0 3.4 fusion.19
  244.6 10.0 scatter_custom_fusion.1
  254.7 4.4 multiply_convert_fusion.2
  259.1 3.9 all-to-all-start.2
  263.9 21.0 %all-to-all-done.2 = bf16[32,80,512]{2,1,0:T(8,128)(2,1)S(1)} async-done(((bf16[32,80,512]{2,1,0:T(8,128)(2,1)}), bf16[32,80,512]{2,1,0:T(8,128)(2,1)S(1)}, u32[]{:S(2)}, u32[]{:S(2)}) %all-to-all-start.2) | async-done | bytes 2621472 | tf_op jit(solution)/shard_map/all_to_all | solution.py:184
  287.2 28.2 %convert_reduce_fusion = (f32[16,2048]{1,0:T(8,128)}, bf16[16,160,2048]{2,1,0:T(8,128)(2,1)}) fusion(f32[16,160,2048]{2,1,0:T(8,128)} %fusion.122, f32[16,2048]{1,0:T(8,128)S(1)} %convert_element_type.159, bf16[16,160,512]{2,1,0:T(8,128)(2,1)} %bitcast.108, bf16[16,2048,512]{2,1,0:T(8,128)(2,1)} %param.36), kind=kOutput, calls=%fused_computation.16 | convolution fusion | flops 5489262592 | bytes 67895296 | tf_op jit(solution)/shard_map/esd,efd->esf/dot_general | solution.py:185
  315.4 18.8 convolution_convert_fusion
  334.2 3.0 copy.83
  337.1 5.2 all-to-all-start.3
  342.4 54.9 %all-reduce.10 = (f32[32]{0:T(128)S(1)}, f32[]{:T(128)}, f32[32]{0:T(128)S(1)}) all-reduce(f32[32]{0:T(128)S(1)} %fusion.87, f32[]{:T(128)} %convert_reduce_fusion.5, f32[32]{0:T(128)S(1)} %get-tuple-element.24), channel_id=1, replica_groups=mesh['rep'=16,'fsdp'=2] {'rep','fsdp'}, use_global_device_ids=true, to_apply=%region_16.17 | all-reduce | flops 65 | bytes 520 | tf_op jit(solution)/shard_map/psum | solution.py:73
  402.7 3.9 multiply_reduce_fusion.3
  406.6 3.2 copy.84
  409.8 9.1 gather_fusion.3
  418.9 3.9 reshape.410
  422.9 2.8 multiply_reduce_fusion.2
  437.4 6.1 fusion.33
  443.5 16.0 multiply_convert_fusion.1
  459.5 4.7 fusion.64
  464.2 4.2 copy.95
  468.3 3.1 reshape.407
  471.5 4.2 fusion.74
  475.6 4.0 copy.89
  479.6 4.0 reshape.405
  483.6 4.7 fusion.79
  488.3 3.2 copy.92
  497.3 3.6 fusion.107
  506.8 36.9 %reduce-scatter.10.cloned.1.call-done = f32[256,1536]{1,0:T(8,128)} async-done(((f32[512,1536]{1,0:T(8,128)}), f32[256,1536]{1,0:T(8,128)}) %reduce-scatter.10.cloned.1.call-update) | async-done | bytes 1572880 | tf_op jit(solution)/shard_map/reduce_scatter | solution.py:289
  543.9 30.2 %fusion.111 = f32[16,2048,512]{2,1,0:T(8,128)} fusion(bf16[16,160,512]{2,1,0:T(8,128)(2,1)S(1)} %bitcast.109, f32[16,160,2048]{2,1,0:T(8,128)} %fusion.122, f32[16,2048]{1,0:T(8,128)S(1)} %convert_element_type.159), kind=kOutput, calls=%fused_computation.184 | convolution fusion | flops 5421137920 | bytes 90832896 | tf_op jit(solution)/shard_map/esf,esd->efd/dot_general | solution.py:206
  575.8 27.5 %fusion.124 = f32[16,512,2048]{2,1,0:T(8,128)} fusion(bf16[16,160,512]{2,1,0:T(8,128)(2,1)S(1)} %bitcast.104, bf16[16,160,2048]{2,1,0:T(8,128)(2,1)} %get-tuple-element.48), kind=kOutput, calls=%fused_computation.194 | convolution fusion | flops 5368709120 | bytes 80216064 | tf_op jit(solution)/shard_map/esd,esf->edf/dot_general | solution.py:202
  609.6 3.9 fusion.112
  616.0 6.9 all-reduce.13
  623.4 60.4 %all-reduce.11 = (f32[256]{0:T(256)}, f32[256]{0:T(256)}, f32[256]{0:T(256)}, f32[256]{0:T(256)}, f32[256]{0:T(256)}, /*index=5*/f32[256]{0:T(256)}, f32[256]{0:T(256)}, f32[256,32]{0,1:T(8,128)}) all-reduce(f32[256]{0:T(256)S(1)} %dynamic-slice.1, f32[256]{0:T(256)S(1)} %dynamic-slice.3, ...), channel_id=1, replica_groups=mesh['rep'=16,'fsdp'=2] {'rep'}, use_global_device_ids=true, to_apply=%region_33.34 | all-reduce | flops 9984 | bytes 79872 | tf_op jit(solution)/shard_map/psum | solution.py:298
  683.7 3.7 add_add_fusion.2
  687.4 84.5 %all-reduce.16.cloned.1.call-done = (f32[256,1536]{1,0:T(8,128)}, f32[256,512]{1,0:T(8,128)}) async-done(((f32[256,1536]{1,0:T(8,128)}, f32[256,512]{1,0:T(8,128)}), (f32[256,1536]{1,0:T(8,128)}, f32[256,512]{1,0:T(8,128)})) %all-reduce.16.cloned.1.call-update) | async-done | bytes 2097168 | tf_op jit(solution)/shard_map/psum | solution.py:298
  771.9 640.9 %reduce-scatter.20.cloned.1.call-done = f32[16,128,512]{2,1,0:T(8,128)} async-done(((f32[16,2048,512]{2,1,0:T(8,128)}), f32[16,128,512]{2,1,0:T(8,128)}) %reduce-scatter.20.cloned.1.call-update) | async-done | bytes 4194320 | tf_op jit(solution)/shard_map/reduce_scatter | solution.py:213
  1412.9 640.6 %reduce-scatter.16.cloned.1.call-done = f32[16,512,128]{2,1,0:T(8,128)} async-done(((f32[16,512,2048]{2,1,0:T(8,128)}), f32[16,512,128]{2,1,0:T(8,128)}) %reduce-scatter.16.cloned.1.call-update) | async-done | bytes 4194320 | tf_op jit(solution)/shard_map/reduce_scatter | solution.py:211
  (268 shorter events, 68.3 us)
Async XLA Ops:
  7.2 13.4 copy-start.56
  7.2 18.6 copy-start.57
  7.2 22.8 %copy-start.58 = (bf16[256]{0:T(256)(128)(2,1)S(1)}, bf16[256]{0:T(256)(128)(2,1)}, u32[]{:S(2)}) copy-start(bf16[256]{0:T(256)(128)(2,1)} %param.27) | copy-start | bytes 1540
  7.2 27.1 %copy-start.59 = (bf16[256]{0:T(256)(128)(2,1)S(1)}, bf16[256]{0:T(256)(128)(2,1)}, u32[]{:S(2)}) copy-start(bf16[256]{0:T(256)(128)(2,1)} %param.28) | copy-start | bytes 1540
  7.2 31.4 %copy-start.60 = (bf16[256]{0:T(256)(128)(2,1)S(1)}, bf16[256]{0:T(256)(128)(2,1)}, u32[]{:S(2)}) copy-start(bf16[256]{0:T(256)(128)(2,1)} %param.30) | copy-start | bytes 1540
  7.2 35.7 %copy-start.61 = (bf16[256]{0:T(256)(128)(2,1)S(1)}, bf16[256]{0:T(256)(128)(2,1)}, u32[]{:S(2)}) copy-start(bf16[256]{0:T(256)(128)(2,1)} %param.31) | copy-start | bytes 1540
  7.3 39.9 %copy-start.62 = (bf16[256]{0:T(256)(128)(2,1)S(1)}, bf16[256]{0:T(256)(128)(2,1)}, u32[]{:S(2)}) copy-start(bf16[256]{0:T(256)(128)(2,1)} %param.32) | copy-start | bytes 1540
  7.3 54.3 %copy-start.35 = (bf16[256,512]{1,0:T(8,128)(2,1)S(1)}, bf16[256,512]{1,0:T(8,128)(2,1)}, u32[]{:S(2)}) copy-start(bf16[256,512]{1,0:T(8,128)(2,1)} %param.29) | copy-start | bytes 786436
  7.3 61.4 %copy-start.5 = (bf16[985,512]{1,0:T(8,128)(2,1)S(1)}, bf16[985,512]{1,0:T(8,128)(2,1)}, u32[]{:S(2)}) copy-start(bf16[985,512]{1,0:T(8,128)(2,1)} %param.19) | copy-start | bytes 3025924
  7.3 62.2 %all-gather.9.cloned.1.call-start = ((), (), s32[]{:S(2)}) async-start(), calls=%async_computation.11 | async-start | bytes 2359296 | tf_op jit(solution)/shard_map/all_gather | solution.py:77
  25.8 47.0 %copy-start.40 = (f32[2,1,256]{2,1,0:T(1,128)}, f32[2,1,256]{2,1,0:T(1,128)S(1)}, u32[]{:S(2)}) copy-start(f32[2,1,256]{2,1,0:T(1,128)S(1)} %convert_element_type.186) | copy-start | bytes 6148
  30.1 42.8 %copy-start.45 = (f32[2,1,256]{2,1,0:T(1,128)}, f32[2,1,256]{2,1,0:T(1,128)S(1)}, u32[]{:S(2)}) copy-start(f32[2,1,256]{2,1,0:T(1,128)S(1)} %convert_element_type.187) | copy-start | bytes 6148
  47.2 59.5 %copy-start.51 = (f32[2,1,256]{2,1,0:T(1,128)}, f32[2,1,256]{2,1,0:T(1,128)S(1)}, u32[]{:S(2)}) copy-start(f32[2,1,256]{2,1,0:T(1,128)S(1)} %convert_element_type.189) | copy-start | bytes 6148
  69.0 3.9 copy-start.31
  69.5 3.4 copy-start.47
  69.5 3.3 copy-start.36
  77.5 19.1 copy-start.8
  89.1 3.1 copy-start
  92.3 4.2 copy-start.33
  106.2 2.7 copy-start.38
  106.6 10.5 copy-start.49
  106.7 10.4 copy-start.42
  117.1 4.2 copy-start.53
  117.1 4.3 copy-start.44
  117.1 28.0 %all-to-all-start = ((bf16[32,80,512]{2,1,0:T(8,128)(2,1)}), bf16[32,80,512]{2,1,0:T(8,128)(2,1)S(1)}, u32[]{:S(2)}, u32[]{:S(2)}) async-start(bf16[32,80,512]{2,1,0:T(8,128)(2,1)} %bitcast.110), calls=%async_computation | async-start | bytes 5242880 | tf_op jit(solution)/shard_map/all_to_all | solution.py:154
  148.6 20.5 copy-start.3
  199.6 5.3 copy-start.24
  199.6 29.1 %all-to-all-start.1 = ((bf16[16,160,512]{2,0,1:T(8,128)(2,1)}), bf16[16,160,512]{2,0,1:T(8,128)(2,1)}, u32[]{:S(2)}, u32[]{:S(2)}) async-start(bf16[16,160,512]{2,0,1:T(8,128)(2,1)} %copy.80), calls=%async_computation.1 | async-start | bytes 5242880 | tf_op jit(solution)/shard_map/all_to_all | solution.py:165
  206.5 7.6 copy-start.54
  206.6 21.5 %copy-start.23 = (bf16[985,512]{1,0:T(8,128)(2,1)S(1)}, bf16[985,512]{1,0:T(8,128)(2,1)}, u32[]{:S(2)}) copy-start(bf16[985,512]{1,0:T(8,128)(2,1)} %copy-done.22) | copy-start | bytes 3025924
  259.1 25.9 %all-to-all-start.2 = ((bf16[32,80,512]{2,1,0:T(8,128)(2,1)}), bf16[32,80,512]{2,1,0:T(8,128)(2,1)S(1)}, u32[]{:S(2)}, u32[]{:S(2)}) async-start(bf16[32,80,512]{2,1,0:T(8,128)(2,1)} %multiply_convert_fusion.2), calls=%async_computation.2 | async-start | bytes 5242880 | tf_op jit(solution)/shard_map/all_to_all | solution.py:184
  284.9 2.3 copy-start.10
  337.1 63.0 %copy-start.15 = (bf16[1970,512]{1,0:T(8,128)(2,1)S(1)}, bf16[1970,512]{1,0:T(8,128)(2,1)}, u32[]{:S(2)}) copy-start(bf16[1970,512]{1,0:T(8,128)(2,1)} %gather_fusion.1) | copy-start | bytes 6051844
  337.1 69.5 %all-to-all-start.3 = ((bf16[16,160,512]{2,0,1:T(8,128)(2,1)}), bf16[16,160,512]{2,0,1:T(8,128)(2,1)}, u32[]{:S(2)}, u32[]{:S(2)}) async-start(bf16[16,160,512]{2,0,1:T(8,128)(2,1)} %copy.83), calls=%async_computation.3 | async-start | bytes 5242880 | tf_op jit(solution)/shard_map/all_to_all | solution.py:193
  342.4 164.5 %reduce-scatter.12.cloned.1.call-start = ((), (), s32[]{:S(2)}) async-start(), calls=%async_computation.13 | async-start | bytes 1572864 | tf_op jit(solution)/shard_map/reduce_scatter | solution.py:292
  422.8 2.8 copy-start.2
  422.8 2.8 copy-start.39
  422.9 2.8 copy-start.43
  422.9 2.8 copy-start.52
  427.2 3.3 copy-start.25
  429.3 1.9 copy-start.29
  434.7 2.7 copy-start.9
  434.7 109.0 %reduce-scatter.10.cloned.1.call-start = ((), (), s32[]{:S(2)}) async-start(), calls=%async_computation.12 | async-start | bytes 4718592 | tf_op jit(solution)/shard_map/reduce_scatter | solution.py:289
  437.4 6.1 copy-start.34
  443.5 16.0 copy-start.19
  464.2 7.3 copy-start.18
  475.6 8.0 copy-start.17
  493.9 3.4 copy-start.6
  493.9 3.4 copy-start.32
  493.9 3.4 copy-start.37
  493.9 3.4 copy-start.41
  493.9 3.4 copy-start.46
  501.0 104.9 %reduce-scatter.22.cloned.1.call-start = ((), (), s32[]{:S(2)}) async-start(), calls=%async_computation.18 | async-start | bytes 278528
  503.1 40.8 %copy-start.20 = (bf16[16,2,80,512]{3,2,1,0:T(8,128)(2,1)S(1)}, bf16[16,2,80,512]{3,2,1,0:T(8,128)(2,1)}, u32[]{:S(2)}) copy-start(bf16[16,2,80,512]{3,2,1,0:T(8,128)(2,1)} %copy.82) | copy-start | bytes 7864324
  503.9 119.4 %reduce-scatter.14.cloned.1.call-start = ((), (), s32[]{:S(2)}) async-start(), calls=%async_computation.14 | async-start | bytes 98304 | tf_op jit(solution)/shard_map/reduce_scatter | solution.py:296
  506.2 181.2 %reduce-scatter.18.cloned.1.call-start = ((), (), s32[]{:S(2)}) async-start(), calls=%async_computation.16 | async-start | bytes 139264 | tf_op jit(solution)/shard_map/reduce_scatter | solution.py:212
  506.8 265.1 %all-reduce.16.cloned.1.call-start = ((), (), s32[]{:S(2)}) async-start(), calls=%async_computation.19 | async-start | bytes 4194304 | tf_op jit(solution)/shard_map/psum | solution.py:298
  543.8 869.0 %reduce-scatter.20.cloned.1.call-start = ((), (), s32[]{:S(2)}) async-start(), calls=%async_computation.17 | async-start | bytes 71303168 | tf_op jit(solution)/shard_map/reduce_scatter | solution.py:213
  574.0 1479.4 %reduce-scatter.16.cloned.1.call-start = ((), (), s32[]{:S(2)}) async-start(), calls=%async_computation.15 | async-start | bytes 71303168 | tf_op jit(solution)/shard_map/reduce_scatter | solution.py:211
  603.3 6.3 copy-start.7
  603.3 6.3 copy-start.55
  609.6 3.9 copy-start.48
  613.5 70.2 %copy-start.14 = (f32[985,512]{1,0:T(8,128)S(1)}, f32[985,512]{1,0:T(8,128)}, u32[]{:S(2)}) copy-start(f32[985,512]{1,0:T(8,128)} %copy-done.13) | copy-start | bytes 6051844
  771.9 1284.2 %copy-start.30 = (f32[256,512]{1,0:T(8,128)S(1)}, f32[256,512]{1,0:T(8,128)}, u32[]{:S(2)}) copy-start(f32[256,512]{1,0:T(8,128)} %get-tuple-element.92) | copy-start | bytes 1572868
  (13 other events, 17.7 us)
Sparse Core Ops, SparseCore 0:
  9.7 30.0 all-gather.8
  434.9 19.6 reduce-scatter.11
  501.1 42.6 reduce-scatter.9
  547.7 55.3 reduce-scatter.21
  605.7 8.8 reduce-scatter.13
  618.4 52.2 reduce-scatter.17
  674.8 97.0 all-reduce.15
  776.7 636.0 reduce-scatter.19
  1417.7 635.6 reduce-scatter.15
where the time goes:
time: 2070 us
  waiting for transfers between devices  1450 us (70%)
  matrix products  196 us (9%)
  blocking collectives  174 us (8%)
  local copies, waits for them, and re-layouts  145 us (7%)
  other arithmetic  61.8 us (3%)
    reduce_scatter x1, waiting for transfers between devices, shards(): lax.psum_scatter(local_out, 'rep', scatter_dimension=1, tiled=True)  641 us
    reduce_scatter x1, waiting for transfers between devices, shards(): lax.psum_scatter(local_in, 'rep', scatter_dimension=2, tiled=True)  641 us
    psum x1, waiting for transfers between devices, shards(): lax.psum((shares[0], shares[1], shares[2], shares[3], shares[4], shares[5...  84.5 us
    psum x1, blocking collectives, shards(): lax.psum((shares[0], shares[1], shares[2], shares[3], shares[4], shares[5...  60.4 us
    psum x1, blocking collectives, shards(): load_total, live_total = lax.psum((load_local, live_local), ('rep', 'fsdp'))  54.9 us
  transfers between devices with their start and end apart: 13, of which 6 were waited for; matrix products, arithmetic and copies ran while one was open for 9% of the time, Pallas kernels for 0%

commit v1 on v0

--- a/solution.py
+++ b/solution.py
@@ -1,6 +1,10 @@
+import functools
+
 import jax
 import jax.numpy as jnp
 from jax import lax
+from jax.experimental import pallas as pl
+from jax.experimental.pallas import tpu as pltpu
 from jax.sharding import PartitionSpec as P
 
 HEADS = 8
@@ -33,10 +37,195 @@
     target = jnp.where(kept_pairs, pair_slot, EXPERTS * CAP)
     slot_owner = slot_owner.at[target].set(pair_token, mode="drop")
     safe_slot = jnp.where(kept_pairs, pair_slot, 0)
-    return (slot_owner, kept_pairs, safe_slot, target, onehot)
+    return (slot_owner, kept_pairs, safe_slot, target, onehot, pair_slot)
+
+
+def expert_grads_by_sum(received, grad_raised_low, active_low, grad_received):
+    local_in = jnp.einsum(
+        "esd,esf->edf", received, grad_raised_low, preferred_element_type=jnp.float32
+    )
+    local_in_bias = jnp.sum(grad_raised_low.astype(jnp.float32), axis=1)
+    local_out = jnp.einsum(
+        "esf,esd->efd", active_low, grad_received, preferred_element_type=jnp.float32
+    )
+    local_out_bias = jnp.sum(grad_received.astype(jnp.float32), axis=1)
+    grad_in_weight, grad_in_bias, grad_out_weight, grad_out_expert_bias = (
+        lax.psum_scatter(local_in, "rep", scatter_dimension=2, tiled=True),
+        lax.psum_scatter(local_in_bias, "rep", scatter_dimension=1, tiled=True),
+        lax.psum_scatter(local_out, "rep", scatter_dimension=1, tiled=True),
+        lax.psum_scatter(local_out_bias, "rep", scatter_dimension=1, tiled=True),
+    )
+    return grad_in_weight, grad_in_bias, grad_out_weight, grad_out_expert_bias
+
+
+def expert_grads_by_slice(
+    rows, cots, kept_pairs, pair_slot, slot_gate, first, first_bias, second
+):
+    axes = ("rep", "fsdp")
+    device = lax.axis_index("rep")
+    core = device % 2
+    local = first.shape[0]
+    total, width = rows.shape
+    groups = [[i for i in range(32) if (i >> 1) % 2 == c] for c in (0, 1)]
+    pad = -total % 16
+
+    def spread(value):
+        return lax.all_gather(value, axes, axis=0, tiled=False, axis_index_groups=groups)
+
+    ids = jnp.where(kept_pairs, pair_slot, -1).reshape(2, total)
+    ids_all = spread(jnp.pad(ids, ((0, 0), (0, pad)), constant_values=-1))
+    cots_all = spread(jnp.pad(cots, ((0, pad), (0, 0))))
+    rows_all = spread(jnp.pad(rows, ((0, pad), (0, 0))))
+    gates_all = spread(slot_gate.reshape(2, local, CAP))
+    mine = lax.axis_index("fsdp")
+    gates_mine = lax.dynamic_index_in_dim(gates_all, mine, axis=1, keepdims=False)
+    gates_mine = gates_mine.transpose(1, 0, 2).reshape(local, 1, -1)
+    base = (mine * (local * CAP)).reshape(1)
+    row_slots = gather_slots(base, rows_all, ids_all, local, CAP)
+    cot_slots = gather_slots(base, cots_all, ids_all, local, CAP)
+    where = jnp.stack([device // 2, core]).astype(jnp.int32)
+    keep_in, send_in, keep_out, send_out, d_bias, d_out_bias = slice_grads(
+        where, row_slots, cot_slots, gates_mine, first, first_bias, second
+    )
+    swap = [(i, i ^ 1) for i in range(16)]
+    got_in, got_out, got_bias, got_out_bias = (
+        lax.ppermute(v, "rep", swap) for v in (send_in, send_out, d_bias, d_out_bias)
+    )
+    bias = (d_bias + got_bias)[:, 0]
+    out_bias = (d_out_bias + got_out_bias)[:, 0]
+    half = bias.shape[1] // 2
+    piece = width // 16
+    return (
+        keep_in + got_in.astype(jnp.float32),
+        lax.dynamic_slice_in_dim(bias, core * half, half, axis=1),
+        keep_out + got_out.astype(jnp.float32),
+        lax.dynamic_slice_in_dim(out_bias, device * piece, piece, axis=1),
+    )
+
+
+def gather_body(base_ref, rows_ref, ids_ref, out_ref):
+    experts, _, cap, width = out_ref.shape
+    slots = experts * cap
+    tokens = rows_ref.shape[1]
+    slot = lax.broadcasted_iota(jnp.int32, (slots, tokens), 0) + base_ref[0]
+    ids = ids_ref[0]
+    hit = (slot == ids[0:1, :]) | (slot == ids[1:2, :])
+    pick = jnp.where(hit, 1.0, 0.0).astype(jnp.bfloat16)
+    got = jnp.dot(pick, rows_ref[0], preferred_element_type=jnp.float32)
+    out_ref[...] = got.astype(jnp.bfloat16).reshape(experts, 1, cap, width)
+
+
+def gather_slots(base, rows, ids, experts, cap):
+    senders, tokens, width = rows.shape
+    return pl.pallas_call(
+        gather_body,
+        grid_spec=pltpu.PrefetchScalarGridSpec(
+            num_scalar_prefetch=1,
+            grid=(senders,),
+            in_specs=[
+                pl.BlockSpec((1, tokens, width), lambda d, b: (d, 0, 0)),
+                pl.BlockSpec((1, 2, tokens), lambda d, b: (d, 0, 0)),
+            ],
+            out_specs=pl.BlockSpec((experts, 1, cap, width), lambda d, b: (0, d, 0, 0)),
+        ),
+        out_shape=jax.ShapeDtypeStruct((experts, senders, cap, width), jnp.bfloat16),
+        cost_estimate=pl.CostEstimate(
+            flops=2 * senders * experts * cap * tokens * width,
+            bytes_accessed=2 * senders * (tokens + experts * cap) * width,
+            transcendentals=0,
+        ),
+        name="gather_slots",
+    )(base, rows, ids)
+
+
+def gelu_pair(value):
+    root = 0.7978845608028654
+    square = value * value
+    bend = jnp.tanh(root * value * (1.0 + 0.044715 * square))
+    half = 0.5 * (1.0 + bend)
+    slope = half + 0.5 * value * (1.0 - bend * bend) * root * (1.0 + 3 * 0.044715 * square)
+    return value * half, slope
+
+
+def slice_grads_body(
+    where_ref, row_ref, cot_ref, gate_ref, in_ref, in_bias_ref, out_ref, keep_in, send_in, keep_out, send_out, d_bias, d_out_bias
+):
+    core = where_ref[1]
+    width = row_ref.shape[-1]
+    rows = row_ref[...].reshape(-1, width)
+    gate = jnp.transpose(jnp.broadcast_to(gate_ref[0], (8, rows.shape[0])))[:, 0:1]
+    grads = (cot_ref[...].reshape(-1, width).astype(jnp.float32) * gate).astype(jnp.bfloat16)
+    first = in_ref[0]
+    second = out_ref[0]
+    raised = jnp.dot(rows, first, preferred_element_type=jnp.float32) + in_bias_ref[0].astype(
+        jnp.float32
+    )
+    active, slope = gelu_pair(raised)
+    active = active.astype(jnp.bfloat16)
+    back = lax.dot_general(
+        grads, second, (((1,), (1,)), ((), ())), preferred_element_type=jnp.float32
+    )
+    draised = (back * slope).astype(jnp.bfloat16)
+    over_rows = (((0,), (0,)), ((), ()))
+    g_in = lax.dot_general(rows, draised, over_rows, preferred_element_type=jnp.float32)
+    g_out = lax.dot_general(active, grads, over_rows, preferred_element_type=jnp.float32)
+    half = g_in.shape[1] // 2
+    first_core = core == 0
+    keep_in[0] = jnp.where(first_core, g_in[:, :half], g_in[:, half:])
+    send_in[0] = jnp.where(first_core, g_in[:, half:], g_in[:, :half]).astype(jnp.bfloat16)
+    keep_out[0] = jnp.where(first_core, g_out[:half], g_out[half:])
+    send_out[0] = jnp.where(first_core, g_out[half:], g_out[:half]).astype(jnp.bfloat16)
+    d_bias[0] = jnp.sum(draised.astype(jnp.float32), axis=0, keepdims=True)
+    d_out_bias[0] = jnp.sum(grads.astype(jnp.float32), axis=0, keepdims=True)
+
+
+def slice_grads(where, rows, cots, gates, first, first_bias, second):
+    experts, senders, cap, width = rows.shape
+    hidden = first.shape[2]
+    part = 256
+    half = part // 2
+    f32 = jnp.float32
+    return pl.pallas_call(
+        slice_grads_body,
+        grid_spec=pltpu.PrefetchScalarGridSpec(
+            num_scalar_prefetch=1,
+            grid=(experts,),
+            in_specs=[
+                pl.BlockSpec((1, senders, cap, width), lambda e, w: (e, 0, 0, 0)),
+                pl.BlockSpec((1, senders, cap, width), lambda e, w: (e, 0, 0, 0)),
+                pl.BlockSpec((1, 1, senders * cap), lambda e, w: (e, 0, 0)),
+                pl.BlockSpec((1, width, part), lambda e, w: (e, 0, w[0])),
+                pl.BlockSpec((1, 1, part), lambda e, w: (e, 0, w[0])),
+                pl.BlockSpec((1, part, width), lambda e, w: (e, w[0], 0)),
+            ],
+            out_specs=[
+                pl.BlockSpec((1, width, half), lambda e, w: (e, 0, 0)),
+                pl.BlockSpec((1, width, half), lambda e, w: (e, 0, 0)),
+                pl.BlockSpec((1, half, width), lambda e, w: (e, 0, 0)),
+                pl.BlockSpec((1, half, width), lambda e, w: (e, 0, 0)),
+                pl.BlockSpec((1, 1, part), lambda e, w: (e, 0, 0)),
+                pl.BlockSpec((1, 1, width), lambda e, w: (e, 0, 0)),
+            ],
+        ),
+        out_shape=[
+            jax.ShapeDtypeStruct((experts, width, half), f32),
+            jax.ShapeDtypeStruct((experts, width, half), jnp.bfloat16),
+            jax.ShapeDtypeStruct((experts, half, width), f32),
+            jax.ShapeDtypeStruct((experts, half, width), jnp.bfloat16),
+            jax.ShapeDtypeStruct((experts, 1, part), f32),
+            jax.ShapeDtypeStruct((experts, 1, width), f32),
+        ],
+        cost_estimate=pl.CostEstimate(
+            flops=8 * experts * senders * cap * width * part,
+            bytes_accessed=4 * experts * (senders * cap * width + 3 * width * part),
+            transcendentals=experts * senders * cap * part,
+        ),
+        name="slice_grads",
+    )(where, rows, cots, gates, first, first_bias.reshape(experts, 1, hidden), second)
 
 
 def shards(
+    fast,
     tokens,
     cotangent,
     routes,
@@ -64,7 +253,7 @@
     image_rows = jnp.arange(rows_count, dtype=jnp.int32) // IMG_TOK
     alive_mask = image_rows < image_count[0]
     alive_float = alive_mask.astype(jnp.float32)[:, None]
-    slot_owner, kept_pairs, safe_slot, target, onehot = slot_table(
+    slot_owner, kept_pairs, safe_slot, target, onehot, pair_slot = slot_table(
         routes, alive_mask, capacity[0], rows_count
     )
     kept_float = kept_pairs.astype(jnp.float32)
@@ -199,20 +388,14 @@
         ),
         axis=0,
     )
-    local_in = jnp.einsum(
-        "esd,esf->edf", received, grad_raised_low, preferred_element_type=jnp.float32
-    )
-    local_in_bias = jnp.sum(grad_raised_low.astype(jnp.float32), axis=1)
-    local_out = jnp.einsum(
-        "esf,esd->efd", active_low, grad_received, preferred_element_type=jnp.float32
-    )
-    local_out_bias = jnp.sum(grad_received.astype(jnp.float32), axis=1)
-    grad_in_weight, grad_in_bias, grad_out_weight, grad_out_expert_bias = (
-        lax.psum_scatter(local_in, "rep", scatter_dimension=2, tiled=True),
-        lax.psum_scatter(local_in_bias, "rep", scatter_dimension=1, tiled=True),
-        lax.psum_scatter(local_out, "rep", scatter_dimension=1, tiled=True),
-        lax.psum_scatter(local_out_bias, "rep", scatter_dimension=1, tiled=True),
-    )
+    if fast:
+        grad_in_weight, grad_in_bias, grad_out_weight, grad_out_expert_bias = expert_grads_by_slice(
+            second_low, cotangent, kept_pairs, pair_slot, slot_gate, expert_in, expert_in_bias, expert_out
+        )
+    else:
+        grad_in_weight, grad_in_bias, grad_out_weight, grad_out_expert_bias = expert_grads_by_sum(
+            received, grad_raised_low, active_low, grad_received
+        )
     prob_local = jnp.sum(router_probs * alive_float, axis=0)
     prob_total = lax.psum(prob_local, ("rep", "fsdp"))
     share = load_total / (2.0 * live_total)
@@ -358,4 +541,5 @@
         P("fsdp", "rep", None),
         P("fsdp", "rep"),
     )
-    return jax.shard_map(shards, mesh=mesh, in_specs=in_specs, out_specs=out_specs, check_vma=False)
+    fast = mesh.shape["rep"] == 16 and mesh.shape["fsdp"] == 2
+    return jax.shard_map(functools.partial(shards, fast), mesh=mesh, in_specs=in_specs, out_specs=out_specs, check_vma=False)

time: 2070 us -> 892 us (0.43)
  waiting for transfers between devices: 1450 us -> 124 us
  blocking collectives: 174 us -> 276 us
  Pallas kernels: 0 us -> 98.7 us
  matrix products: 196 us -> 131 us
    reduce_scatter x3 -> x0, waiting for transfers between devices: 1280 us -> none  [the longest x1 641 us: shards(): lax.psum_scatter(local_out, 'rep', scatter_dimension=1, tiled=True)]
    pallas_call x0 -> x3, Pallas kernels: none -> 98.7 us  [the longest x2 56.9 us: gather_slots(): pl.pallas_call(gather_body, grid_spec=pltpu.PrefetchScalarGridSpec(num_sc...]
    all_gather x0 -> x2, blocking collectives: none -> 97.3 us  [spread(): lax.all_gather(value, axes, axis=0, tiled=False, axis_index_groups=groups)]
    dot_general x3 -> x0, matrix products: 85.8 us -> none  [the longest x1 30.2 us: shards(): jnp.einsum('esf,esd->efd', active_low, grad_received, preferred_element_t...]
    reduce_scatter x1, waiting for transfers between devices: 36.9 us -> 0.01 us  [shards(): lax.psum_scatter(local_grads[2], 'fsdp', scatter_dimension=0, tiled=True)]
    all_to_all x1, waiting for transfers between devices: 21 us -> 0.01 us  [shards(): lax.all_to_all(slot_grads, 'fsdp', split_axis=0, concat_axis=1, tiled=True)]
  transfers between devices with their start and end apart: 13 -> 15, of which waited for: 6 -> 3; matrix products, arithmetic and copies ran while one was open for 9% -> 38% of each run, Pallas kernels for 0% -> 11%
where the time goes in v1:
time: 892 us; the launch traced here: 885 us
  blocking collectives  276 us (31%)
  local copies, waits for them, and re-layouts  144 us (16%)
  matrix products  131 us (15%)
  waiting for transfers between devices  124 us (14%)
  Pallas kernels  98.7 us (11%)
  other arithmetic  69.9 us (8%)
  starting transfers between devices  21.9 us (2%)
  between operations  20 us (2%)
    all_gather x2, blocking collectives, spread(): lax.all_gather(value, axes, axis=0, tiled=False, axis_index_groups=groups)  97.3 us
    psum x1, waiting for transfers between devices, shards(): lax.psum((shares[0], shares[1], shares[2], shares[3], shares[4], shares[5...  82.3 us
    psum x1, blocking collectives, shards(): load_total, live_total = lax.psum((load_local, live_local), ('rep', 'fsdp'))  64.7 us
    psum x1, blocking collectives, shards(): lax.psum((shares[0], shares[1], shares[2], shares[3], shares[4], shares[5...  58.9 us
    pallas_call x2, Pallas kernels, gather_slots(): pl.pallas_call(gather_body, grid_spec=pltpu.PrefetchScalarGridSpec(num_sc...  56.9 us
    pallas_call x1, Pallas kernels, slice_grads(): pl.pallas_call(slice_grads_body, grid_spec=pltpu.PrefetchScalarGridSpec(n...  41.8 us
    all_to_all x1, waiting for transfers between devices, shards(): lax.all_to_all(sent_rows, 'fsdp', split_axis=0, concat_axis=1, tiled=True)  40.4 us
    dot_general x1, matrix products, shards(): jnp.einsum('esf,edf->esd', grad_raised_low, expert_in, preferred_element_...  36.7 us
  transfers between devices with their start and end apart: 15, of which 3 were waited for; matrix products, arithmetic and copies ran while one was open for 38% of the time, Pallas kernels for 11%

profile of v1, /device:TPU:0, one launch (start us, length us, event | category | flops | bytes accessed | tf_op | source)
XLA Modules:
  0.0 884.8 jit_solution(1664851371269938701)
XLA Ops:
  10.4 5.2 all-gather.7
  15.6 4.2 all-gather.6
  19.9 4.3 all-gather.5
  24.2 4.2 all-gather.4
  28.5 4.3 all-gather.3
  32.7 4.3 all-gather.8
  37.0 4.3 all-gather.9
  41.4 7.2 all_gather.56
  49.9 3.4 add_convert_fusion
  59.3 2.9 reshape.414
  62.2 4.5 multiply_reduce_fusion.1
  69.9 4.2 fusion.15
  76.1 3.2 copy.102
  87.9 9.1 %reduce-window.6 = s32[32,16,128]{2,1,0:T(8,128)S(1)} reduce-window(s32[32,16,128]{2,1,0:T(8,128)S(1)} %bitcast.115, s32[]{:T(128)} %constant.55.clone.1), window={size=1x1x128 pad=0_0x0_0x127_0}, to_apply=%region_6.7 | reduce-window | flops 8323072 | bytes 524292 | tf_op jit(solution)/shard_map/reduce-window
  98.7 10.0 %scatter_custom_fusion = s32[2560]{0:T(1024)S(1)} fusion(s32[1970]{0:T(1024)S(1)} %bitcast.149, s32[1970]{0:T(1024)S(1)} %pad_add_fusion.1, s32[]{:T(128)} %constant.106.clone.1), kind=kCustom, calls=%fused_computation.152 | custom fusion | bytes 10244 | tf_op jit(solution)/shard_map/scatter | solution.py:38
  108.8 8.4 gather_fusion
  117.2 5.1 all-to-all-start
  122.4 40.4 %all-to-all-done = bf16[32,80,512]{2,1,0:T(8,128)(2,1)} async-done(((bf16[32,80,512]{2,1,0:T(8,128)(2,1)}), bf16[32,80,512]{2,1,0:T(8,128)(2,1)}, u32[]{:S(2)}, u32[]{:S(2)}) %all-to-all-start) | async-done | bytes 2621472 | tf_op jit(solution)/shard_map/all_to_all | solution.py:343
  162.8 3.5 copy.105
  166.3 21.1 %fusion.138 = f32[16,160,2048]{2,1,0:T(8,128)} fusion(bf16[16,160,512]{2,1,0:T(8,128)(2,1)} %bitcast.112, bf16[16,512,2048]{2,1,0:T(8,128)(2,1)} %in_ref.1), kind=kOutput, calls=%fused_computation.211 | convolution fusion | flops 5368709120 | bytes 57147392 | tf_op jit(solution)/shard_map/esd,edf->esf/dot_general | solution.py:345
  187.4 26.0 %add_convert_fusion.1 = bf16[16,160,512]{2,1,0:T(8,128)(2,1)} fusion(f32[16,512]{1,0:T(8,128)S(1)} %convert_element_type.163, bf16[16,2048,512]{2,1,0:T(8,128)(2,1)} %out_ref.1, f32[16,160,2048]{2,1,0:T(8,128)} %fusion.138, f32[16,2048]{1,0:T(8,128)S(1)} %convert_element_type.161), kind=kOutput, calls=%fused_computation.30 | convolution fusion | flops 5423759360 | bytes 57311232 | tf_op jit(solution)/shard_map/esf,efd->esd/dot_general | solution.py:351
  213.4 4.7 copy.106
  218.1 5.1 all-to-all-start.1
  225.0 7.6 gather_fusion.2
  232.6 8.6 all_gather.60
  241.9 3.2 copy.107
  245.1 9.5 %gather_fusion.1 = bf16[1970,512]{1,0:T(8,128)(2,1)} fusion(bf16[2560,512]{1,0:T(8,128)(2,1)S(1)} %bitcast.110, s32[2048]{0:T(1024)S(1)} %pad_clamp_fusion.1), kind=kCustom, calls=%fused_computation.1 | custom fusion | bytes 4042440 | tf_op jit(solution)/shard_map/gather | solution.py:357
  254.6 3.4 fusion.22
  258.3 10.0 %scatter_custom_fusion.1 = f32[2560]{0:T(1024)S(1)} fusion(s32[1970]{0:T(1024)S(1)} %bitcast.150, f32[1970]{0:T(1024)S(1)} %maximum_select_fusion, f32[]{:T(128)} %constant.100.clone.1), kind=kCustom, calls=%fused_computation.150 | custom fusion | bytes 10244 | tf_op jit(solution)/shard_map/scatter | solution.py:366
  268.3 4.4 multiply_convert_fusion.3
  272.7 5.1 all-to-all-start.2
  281.6 64.7 %all-reduce.13 = (f32[32]{0:T(128)S(1)}, f32[]{:T(128)}, f32[32]{0:T(128)S(1)}) all-reduce(f32[32]{0:T(128)S(1)} %fusion.93, f32[]{:T(128)} %convert_reduce_fusion.3, f32[32]{0:T(128)S(1)} %get-tuple-element.36), channel_id=1, replica_groups=mesh['rep'=16,'fsdp'=2] {'rep','fsdp'}, use_global_device_ids=true, to_apply=%region_16.17 | all-reduce | flops 65 | bytes 520 | tf_op jit(solution)/shard_map/psum | solution.py:262
  352.3 43.9 %all_gather.67 = f32[16,2,16,80]{3,2,1,0:T(8,128)S(1)} all-gather(f32[1,2,16,80]{3,2,1,0:T(8,128)S(1)} %all_gather_reshape.3), channel_id=1, replica_groups={{0,1,4,5,8,9,12,13,16,17,20,21,24,25,28,29},{2,3,6,7,10,11,14,15,18,19,..., dimensions={0}, use_global_device_ids=true | all-gather | bytes 174080 | tf_op jit(solution)/shard_map/all_gather | solution.py:73
  399.1 36.7 %fusion.33 = bf16[16,160,512]{2,1,0:T(8,128)(2,1)} fusion(bf16[16,512,2048]{2,1,0:T(8,128)(2,1)} %in_ref.1, f32[16,160,2048]{2,1,0:T(8,128)} %fusion.138, f32[16,2048]{1,0:T(8,128)S(1)} %convert_element_type.161, bf16[16,160,512]{2,1,0:T(8,128)(2,1)S(1)} %bitcast.114, bf16[16,2048,512]{2,1,0:T(8,128)(2,1)} %out_ref.1), kind=kOutput, calls=%fused_computation.61 | convolution fusion | flops 10848829440 | bytes 93454336 | tf_op jit(solution)/shard_map/esf,edf->esd/dot_general | solution.py:379
  435.8 4.7 copy.109
  440.5 5.1 all-to-all-start.3
  446.7 53.4 %all-gather.10.ids_ref = s32[16,2,992]{2,1,0:T(2,128)} all-gather(s32[1,2,992]{2,1,0:T(2,128)S(1)} %pad_bitcast_fusion), channel_id=3, replica_groups={{0,1,4,5,8,9,12,13,16,17,20,21,24,25,28,29},{2,3,6,7,10,11,14,15,18,19,..., dimensions={0}, use_global_device_ids=true | all-gather | bytes 134912 | tf_op jit(solution)/shard_map/all_gather | solution.py:73
  500.1 3.9 multiply_reduce_fusion.3
  504.0 3.2 copy.110
  507.2 9.3 %gather_fusion.3 = bf16[1970,512]{1,0:T(8,128)(2,1)} fusion(bf16[2560,512]{1,0:T(8,128)(2,1)S(1)} %bitcast.109, s32[2048]{0:T(1024)S(1)} %pad_clamp_fusion.1), kind=kCustom, calls=%fused_computation.3 | custom fusion | bytes 4042440 | tf_op jit(solution)/shard_map/gather | solution.py:386
  516.5 3.9 reshape.431
  520.5 2.8 multiply_reduce_fusion.2
  530.9 3.8 reshape.422
  534.8 6.1 fusion.39
  540.9 15.7 %multiply_convert_fusion.2 = bf16[8,5,197,197]{2,3,1,0:T(8,128)(2,1)} fusion(f32[8,5,197,197]{2,3,1,0:T(8,128)} %fusion.39, f32[8,5,197,197]{2,3,1,0:T(8,128)} %copy-done, f32[8,5,197]{2,1,0:T(8,128)S(1)} %copy-done.30), kind=kOutput, calls=%fused_computation.19 | output fusion | flops 12426956 | bytes 15555120 | tf_op jit(solution)/shard_map/sub | solution.py:432
  556.6 3.4 fusion.139
  560.1 4.2 fusion.80
  564.2 4.1 copy.115
  568.4 4.0 reshape.423
  572.3 4.7 fusion.85
  577.0 4.0 copy.118
  581.0 4.0 reshape.424
  585.0 4.7 fusion.70
  589.6 3.2 copy.121
  598.8 3.6 fusion.123
  602.6 28.6 %gather_slots.3.cot_ref = bf16[16,16,80,512]{3,2,1,0:T(8,128)(2,1)} custom-call(s32[1]{0:T(128)} %bitcast.37.base_ref, bf16[16,992,512]{2,1,0:T(8,128)(2,1)} %bitcast.158, s32[16,2,992]{2,1,0:T(2,128)} %all-gather.10.ids_ref), custom_call_target="tpu_custom_call" | custom-call | flops 20803747840 | bytes 37224448 | tf_op jit(solution)/shard_map/gather_slots/pallas_call | solution.py:120
  631.2 28.3 %gather_slots.2.row_ref = bf16[16,16,80,512]{3,2,1,0:T(8,128)(2,1)} custom-call(s32[1]{0:T(128)} %bitcast.37.base_ref, bf16[16,992,512]{2,1,0:T(8,128)(2,1)} %bitcast.159, s32[16,2,992]{2,1,0:T(2,128)} %all-gather.10.ids_ref), custom_call_target="tpu_custom_call" | custom-call | flops 20803747840 | bytes 37224448 | tf_op jit(solution)/shard_map/gather_slots/pallas_call | solution.py:120
  659.5 41.8 %slice_grads.1 = (f32[16,512,128]{2,1,0:T(8,128)}, bf16[16,512,128]{2,1,0:T(8,128)(2,1)}, f32[16,128,512]{2,1,0:T(8,128)}, bf16[16,128,512]{2,1,0:T(8,128)(2,1)}...) custom-call(s32[2]{0:T(128)} %pad_add_fusion.3.where_ref, bf16[16,16,80,512]{3,2,1,0:T(8,128)(2,1)} %gather_slots.2.row_ref, ...), custom_call_target="tpu_custom_call" | custom-call | flops 21474836480 | bytes 67108864 | tf_op jit(solution)/shard_map/slice_grads/pallas_call | solution.py:188
  701.4 4.3 fusion.127
  710.9 8.4 all-reduce.16
  719.8 58.9 %all-reduce.14 = (f32[256]{0:T(256)}, f32[256]{0:T(256)}, f32[256]{0:T(256)}, f32[256]{0:T(256)}, f32[256]{0:T(256)}, /*index=5*/f32[256]{0:T(256)}, f32[256]{0:T(256)}, f32[256,32]{0,1:T(8,128)}) all-reduce(f32[256]{0:T(256)S(1)} %dynamic-slice.3, f32[256]{0:T(256)S(1)} %dynamic-slice.5, ...), channel_id=1, replica_groups=mesh['rep'=16,'fsdp'=2] {'rep'}, use_global_device_ids=true, to_apply=%region_33.34 | all-reduce | flops 9984 | bytes 79872 | tf_op jit(solution)/shard_map/psum | solution.py:481
  780.7 5.4 convert_add_fusion.1
  786.2 4.4 convert_add_fusion
  790.6 82.3 %all-reduce.19.cloned.1.call-done = (f32[256,1536]{1,0:T(8,128)}, f32[256,512]{1,0:T(8,128)}) async-done(((f32[256,1536]{1,0:T(8,128)}, f32[256,512]{1,0:T(8,128)}), (f32[256,1536]{1,0:T(8,128)}, f32[256,512]{1,0:T(8,128)})) %all-reduce.19.cloned.1.call-update) | async-done | bytes 2097168 | tf_op jit(solution)/shard_map/psum | solution.py:481
  (282 shorter events, 64.0 us)
Async XLA Ops:
  7.2 3.2 copy-start.54
  7.2 8.4 copy-start.55
  7.2 12.7 %copy-start.56 = (bf16[256]{0:T(256)(128)(2,1)S(1)}, bf16[256]{0:T(256)(128)(2,1)}, u32[]{:S(2)}) copy-start(bf16[256]{0:T(256)(128)(2,1)} %param.27) | copy-start | bytes 1540
  7.2 16.9 %copy-start.57 = (bf16[256]{0:T(256)(128)(2,1)S(1)}, bf16[256]{0:T(256)(128)(2,1)}, u32[]{:S(2)}) copy-start(bf16[256]{0:T(256)(128)(2,1)} %param.25) | copy-start | bytes 1540
  7.2 21.2 %copy-start.58 = (bf16[256]{0:T(256)(128)(2,1)S(1)}, bf16[256]{0:T(256)(128)(2,1)}, u32[]{:S(2)}) copy-start(bf16[256]{0:T(256)(128)(2,1)} %param.24) | copy-start | bytes 1540
  7.2 25.5 %copy-start.59 = (bf16[256]{0:T(256)(128)(2,1)S(1)}, bf16[256]{0:T(256)(128)(2,1)}, u32[]{:S(2)}) copy-start(bf16[256]{0:T(256)(128)(2,1)} %param.31) | copy-start | bytes 1540
  7.3 29.7 %copy-start.60 = (bf16[256]{0:T(256)(128)(2,1)S(1)}, bf16[256]{0:T(256)(128)(2,1)}, u32[]{:S(2)}) copy-start(bf16[256]{0:T(256)(128)(2,1)} %param.32) | copy-start | bytes 1540
  7.3 34.1 %copy-start.31 = (bf16[256,512]{1,0:T(8,128)(2,1)S(1)}, bf16[256,512]{1,0:T(8,128)(2,1)}, u32[]{:S(2)}) copy-start(bf16[256,512]{1,0:T(8,128)(2,1)} %param.29) | copy-start | bytes 786436
  7.3 41.2 %copy-start.3 = (bf16[985,512]{1,0:T(8,128)(2,1)S(1)}, bf16[985,512]{1,0:T(8,128)(2,1)}, u32[]{:S(2)}) copy-start(bf16[985,512]{1,0:T(8,128)(2,1)} %param.19) | copy-start | bytes 3025924
  7.3 42.0 %all-gather.15.cloned.1.call-start = ((), (), s32[]{:S(2)}) async-start(), calls=%async_computation.7 | async-start | bytes 2359296 | tf_op jit(solution)/shard_map/all_gather | solution.py:266
  8.0 594.5 %all-gather.19.cloned.1.call-start = ((), (), s32[]{:S(2)}) async-start(), calls=%async_computation.12 | async-start | bytes 17268736 | tf_op jit(solution)/shard_map/all_gather | solution.py:73
  10.3 620.9 %all-gather.17.cloned.1.call-start = ((), (), s32[]{:S(2)}) async-start(), calls=%async_computation.11 | async-start | bytes 17268736 | tf_op jit(solution)/shard_map/all_gather | solution.py:73
  28.4 20.9 %copy-start.41 = (f32[2,1,256]{2,1,0:T(1,128)}, f32[2,1,256]{2,1,0:T(1,128)S(1)}, u32[]{:S(2)}) copy-start(f32[2,1,256]{2,1,0:T(1,128)S(1)} %convert_element_type.189) | copy-start | bytes 6148
  32.7 16.6 %copy-start.37 = (f32[2,1,256]{2,1,0:T(1,128)}, f32[2,1,256]{2,1,0:T(1,128)S(1)}, u32[]{:S(2)}) copy-start(f32[2,1,256]{2,1,0:T(1,128)S(1)} %convert_element_type.188) | copy-start | bytes 6148
  37.0 48.3 %copy-start.47 = (f32[2,1,256]{2,1,0:T(1,128)}, f32[2,1,256]{2,1,0:T(1,128)S(1)}, u32[]{:S(2)}) copy-start(f32[2,1,256]{2,1,0:T(1,128)S(1)} %convert_element_type.191) | copy-start | bytes 6148
  62.2 12.0 %copy-start.5 = (bf16[5,197,8,64]{3,2,1,0:T(8,128)(2,1)}, bf16[5,197,8,64]{3,2,1,0:T(8,128)(2,1)S(1)}, u32[]{:S(2)}) copy-start(bf16[5,197,8,64]{3,2,1,0:T(8,128)(2,1)S(1)} %reshape.414) | copy-start | bytes 3025924
  66.7 3.2 copy-start
  69.9 4.2 copy-start.29
  84.0 1.7 copy-start.35
  85.3 2.3 copy-start.51
  85.7 155.6 %copy-start.13 = (bf16[985,512]{1,0:T(8,128)(2,1)}, bf16[985,512]{1,0:T(8,128)(2,1)S(1)}, u32[]{:S(2)}) copy-start(bf16[985,512]{1,0:T(8,128)(2,1)S(1)} %add_convert_fusion.2) | copy-start | bytes 3025924
  117.2 5.2 copy-start.32
  117.2 5.2 copy-start.49
  117.2 45.6 %all-to-all-start = ((bf16[32,80,512]{2,1,0:T(8,128)(2,1)}), bf16[32,80,512]{2,1,0:T(8,128)(2,1)}, u32[]{:S(2)}, u32[]{:S(2)}) async-start(bf16[32,80,512]{2,1,0:T(8,128)(2,1)} %bitcast.113), calls=%async_computation | async-start | bytes 5242880 | tf_op jit(solution)/shard_map/all_to_all | solution.py:343
  218.0 5.3 copy-start.15
  218.1 23.9 %all-to-all-start.1 = ((bf16[16,160,512]{2,0,1:T(8,128)(2,1)}), bf16[16,160,512]{2,0,1:T(8,128)(2,1)}, u32[]{:S(2)}, u32[]{:S(2)}) async-start(bf16[16,160,512]{2,0,1:T(8,128)(2,1)} %copy.106), calls=%async_computation.1 | async-start | bytes 5242880 | tf_op jit(solution)/shard_map/all_to_all | solution.py:354
  225.0 7.6 copy-start.50
  272.7 6.2 copy-start.61
  272.7 77.0 %copy-start.10 = (bf16[1970,512]{1,0:T(8,128)(2,1)S(1)}, bf16[1970,512]{1,0:T(8,128)(2,1)}, u32[]{:S(2)}) copy-start(bf16[1970,512]{1,0:T(8,128)(2,1)} %gather_fusion.1) | copy-start | bytes 6051844
  272.7 124.4 %all-to-all-start.2 = ((bf16[32,80,512]{2,1,0:T(8,128)(2,1)}), bf16[32,80,512]{2,1,0:T(8,128)(2,1)}, u32[]{:S(2)}, u32[]{:S(2)}) async-start(bf16[32,80,512]{2,1,0:T(8,128)(2,1)} %multiply_convert_fusion.3), calls=%async_computation.2 | async-start | bytes 5242880 | tf_op jit(solution)/shard_map/all_to_all | solution.py:373
  440.5 5.2 copy-start.14
  440.5 63.6 %all-to-all-start.3 = ((bf16[16,160,512]{2,0,1:T(8,128)(2,1)}), bf16[16,160,512]{2,0,1:T(8,128)(2,1)}, u32[]{:S(2)}, u32[]{:S(2)}) async-start(bf16[16,160,512]{2,0,1:T(8,128)(2,1)} %copy.109), calls=%async_computation.3 | async-start | bytes 5242880 | tf_op jit(solution)/shard_map/all_to_all | solution.py:382
  445.6 274.2 %reduce-scatter.8.cloned.1.call-start = ((), (), s32[]{:S(2)}) async-start(), calls=%async_computation.10 | async-start | bytes 98304 | tf_op jit(solution)/shard_map/reduce_scatter | solution.py:479
  446.6 332.1 %reduce-scatter.6.cloned.1.call-start = ((), (), s32[]{:S(2)}) async-start(), calls=%async_computation.9 | async-start | bytes 1572864 | tf_op jit(solution)/shard_map/reduce_scatter | solution.py:475
  520.5 2.8 copy-start.2
  520.5 2.8 copy-start.36
  520.5 2.8 copy-start.40
  520.5 2.8 copy-start.48
  524.9 2.1 copy-start.16
  527.0 2.2 copy-start.25
  529.2 5.5 copy-start.6
  534.8 6.1 copy-start.30
  556.6 3.5 copy-start.18
  560.0 218.7 %reduce-scatter.4.cloned.1.call-start = ((), (), s32[]{:S(2)}) async-start(), calls=%async_computation.8 | async-start | bytes 4718592 | tf_op jit(solution)/shard_map/reduce_scatter | solution.py:472
  564.2 8.1 copy-start.17
  577.0 8.0 copy-start.19
  595.3 1.8 copy-start.23
  595.3 3.5 copy-start.4
  595.3 3.5 copy-start.28
  595.3 3.5 copy-start.34
  595.3 3.5 copy-start.38
  595.3 3.5 copy-start.42
  602.5 270.3 %all-reduce.19.cloned.1.call-start = ((), (), s32[]{:S(2)}) async-start(), calls=%async_computation.13 | async-start | bytes 4194304 | tf_op jit(solution)/shard_map/psum | solution.py:481
  701.3 4.4 copy-start.44
  701.3 79.4 %collective-permute-start = (bf16[16,512,128]{2,1,0:T(8,128)(2,1)}, bf16[16,512,128]{2,1,0:T(8,128)(2,1)}, u32[]{:S(2)}, u32[]{:S(2)}) collective-permute-start(bf16[16,512,128]{2,1,0:T(8,128)(2,1)} %get-tuple-element.24), channel_id=1, source_target_pairs={{0,2},{2,0},{4,6},{6,4},{8,10},{10,8},{12,14},{14,12},{16,18},{18,... | collective-permute-start | bytes 6291464 | tf_op jit(solution)/shard_map/ppermute | solution.py:92
  705.6 1.9 copy-start.12
  705.7 80.5 %collective-permute-start.2 = (bf16[16,128,512]{2,1,0:T(8,128)(2,1)}, bf16[16,128,512]{2,1,0:T(8,128)(2,1)}, u32[]{:S(2)}, u32[]{:S(2)}) collective-permute-start(bf16[16,128,512]{2,1,0:T(8,128)(2,1)} %get-tuple-element.27), channel_id=1, source_target_pairs={{0,2},{2,0},{4,6},{6,4},{8,10},{10,8},{12,14},{14,12},{16,18},{18,... | collective-permute-start | bytes 6291464 | tf_op jit(solution)/shard_map/ppermute | solution.py:92
  706.2 2.0 copy-start.9
  708.3 2.3 copy-start.52
  708.3 70.4 %copy-start.53 = (f32[16,1,512]{2,1,0:T(1,128)S(1)}, f32[16,1,512]{2,1,0:T(1,128)}, u32[]{:S(2)}) copy-start(f32[16,1,512]{2,1,0:T(1,128)} %get-tuple-element.28) | copy-start | bytes 98308
  710.6 68.2 %collective-permute-start.1 = (f32[16,1,256]{2,1,0:T(1,128)S(1)}, f32[16,1,256]{2,1,0:T(1,128)S(1)}, u32[]{:S(2)}, u32[]{:S(2)}) collective-permute-start(f32[16,1,256]{2,1,0:T(1,128)S(1)} %copy-done.52), channel_id=1, source_target_pairs={{0,2},{2,0},{4,6},{6,4},{8,10},{10,8},{12,14},{14,12},{16,18},{18,... | collective-permute-start | bytes 49160 | tf_op jit(solution)/shard_map/ppermute | solution.py:92
  778.7 1.3 collective-permute-start.3
  780.7 5.4 copy-start.21
  872.8 2.7 copy-start.26
  (13 other events, 14.5 us)
Sparse Core Ops, SparseCore 0:
  9.7 30.7 all-gather.14
  43.3 196.1 all-gather.18
  242.3 191.9 all-gather.16
  448.3 12.9 reduce-scatter.7
  560.1 17.7 reduce-scatter.5
  602.6 40.8 reduce-scatter.3
  778.8 93.9 all-reduce.18
